TPU v7x, 256 devices: a whole 4x4x8 slice. The times are simulated.
256 devices in a mesh: context: 32 (over x, z), mp: 8 (over y, core).
Axes of the slice: x: 4, y: 4, z: 8, core: 2. Of those that a mesh axis runs over, the one named last changes fastest.
Arguments:
- queries: bfloat16 [32768, 2048], P('context', 'mp'), may hold values from -32 to 32
- keys: bfloat16 [32768, 1024], P('context', 'mp'), may hold values from -32 to 32
- values: bfloat16 [32768, 1024], P('context', 'mp'), may hold values from -6 to 6
- out_grad: bfloat16 [32768, 5376], P(('context', 'mp')), may hold values from -24 to 24
- out_weight: bfloat16 [5376, 2048], P(None, 'mp'), may hold values from -0.125 to 0.125
Outputs:
- query_grad: bfloat16 [32768, 2048], P('context', 'mp')
- key_grad: bfloat16 [32768, 1024], P('context', 'mp')
- value_grad: bfloat16 [32768, 1024], P('context', 'mp')
- weight_grad: bfloat16 [5376, 2048], P('context', 'mp')
All inputs are finite; a program needn't handle non-finite values.
Results may differ from a plain program's by a relative error of at most 0.02.
Values may be sent and summed in bfloat16 or wider, within the bound.
A program may use at most 128 MiB of HBM per device.

v0:
```python
import jax
import jax.numpy as jnp
from jax import lax
from jax.sharding import PartitionSpec as P

HEAD_SIZE = 128
WINDOW_KEYS = 512


SCALE = 168.0 ** (-0.5)
NEG = -1e30


def shifted(x, axis, by):
    devices = lax.axis_size(axis)
    pairs = [(i, i + by) for i in range(devices) if 0 <= i + by < devices]
    return lax.ppermute(x, axis, pairs)


def band_grads(query_rows_block, key_rows_block, value_rows_block, output_grad_rows, key_start):
    rows = query_rows_block.shape[0]
    span = key_rows_block.shape[0]
    scores = (
        jnp.einsum(
            "qhgd,khd->hgqk", query_rows_block, key_rows_block, preferred_element_type=jnp.float32
        )
        * SCALE
    )
    qpos = jnp.arange(rows, dtype=jnp.int32)[:, None]
    kpos = jnp.arange(span, dtype=jnp.int32)[None, :]
    allowed = (kpos > qpos) & (kpos <= qpos + (span - rows)) & (kpos + key_start >= 0)
    scores = jnp.where(allowed, scores, NEG)
    top = jnp.max(scores, axis=-1, keepdims=True)
    weights = jnp.exp(scores - top)
    prob = weights / jnp.sum(weights, axis=-1, keepdims=True)
    prob_b = prob.astype(jnp.bfloat16)
    attn = jnp.einsum(
        "hgqk,khd->qhgd", prob_b, value_rows_block, preferred_element_type=jnp.float32
    ).astype(jnp.bfloat16)
    delta = jnp.sum(output_grad_rows.astype(jnp.float32) * attn.astype(jnp.float32), axis=-1)
    delta = jnp.transpose(delta, (1, 2, 0))[..., None]
    dprob = jnp.einsum(
        "qhgd,khd->hgqk", output_grad_rows, value_rows_block, preferred_element_type=jnp.float32
    )
    dscore = (prob * (dprob - delta) * SCALE).astype(jnp.bfloat16)
    dq = jnp.einsum("hgqk,khd->qhgd", dscore, key_rows_block, preferred_element_type=jnp.float32)
    key_gradient = jnp.einsum(
        "hgqk,qhgd->khd", dscore, query_rows_block, preferred_element_type=jnp.float32
    )
    value_gradient = jnp.einsum(
        "hgqk,qhgd->khd", prob_b, output_grad_rows, preferred_element_type=jnp.float32
    )
    return (dq, attn, key_gradient, value_gradient)


def shards(queries, keys, values, out_grad, out_weight):
    shard = queries.shape[0]
    kv_local = keys.shape[1] // HEAD_SIZE
    q_local = queries.shape[1] // HEAD_SIZE
    query_group = q_local // kv_local
    block_index = WINDOW_KEYS // 2
    root = lax.axis_index("context") * shard - WINDOW_KEYS
    prev_keys, prev_values = shifted((keys, values), "context", 1)
    prev_keys = prev_keys[shard - WINDOW_KEYS :]
    prev_values = prev_values[shard - WINDOW_KEYS :]
    key_buf = jnp.concatenate([prev_keys, keys], 0)
    value_buf = jnp.concatenate([prev_values, values], 0)
    grad_full = lax.all_gather(out_grad, "mp", axis=0, tiled=True)
    output_gradient = jnp.dot(grad_full, out_weight, preferred_element_type=jnp.float32).astype(
        jnp.bfloat16
    )

    def step(index, carry):
        dq_all, attn_all, key_gradient_total, value_gradient_total = carry
        start_position = index * block_index
        query_rows_block = lax.dynamic_slice_in_dim(
            queries, start_position, block_index, 0
        ).reshape(block_index, kv_local, query_group, HEAD_SIZE)
        output_grad_rows = lax.dynamic_slice_in_dim(
            output_gradient, start_position, block_index, 0
        ).reshape(block_index, kv_local, query_group, HEAD_SIZE)
        key_rows_block = lax.dynamic_slice_in_dim(
            key_buf, start_position, WINDOW_KEYS + block_index, 0
        ).reshape(WINDOW_KEYS + block_index, kv_local, HEAD_SIZE)
        value_rows_block = lax.dynamic_slice_in_dim(
            value_buf, start_position, WINDOW_KEYS + block_index, 0
        ).reshape(WINDOW_KEYS + block_index, kv_local, HEAD_SIZE)
        dq, attn, key_gradient, value_gradient = band_grads(
            query_rows_block,
            key_rows_block,
            value_rows_block,
            output_grad_rows,
            root + start_position,
        )
        dq_all = lax.dynamic_update_slice_in_dim(
            dq_all, dq.reshape(block_index, q_local * HEAD_SIZE), start_position, 0
        )
        attn_all = lax.dynamic_update_slice_in_dim(
            attn_all, attn.reshape(block_index, q_local * HEAD_SIZE), start_position, 0
        )
        earlier_keys = lax.dynamic_slice_in_dim(
            key_gradient_total, start_position, WINDOW_KEYS + block_index, 0
        )
        earlier_values = lax.dynamic_slice_in_dim(
            value_gradient_total, start_position, WINDOW_KEYS + block_index, 0
        )
        key_gradient_total = lax.dynamic_update_slice_in_dim(
            key_gradient_total,
            earlier_keys + key_gradient.reshape(WINDOW_KEYS + block_index, kv_local * HEAD_SIZE),
            start_position,
            0,
        )
        value_gradient_total = lax.dynamic_update_slice_in_dim(
            value_gradient_total,
            earlier_values
            + value_gradient.reshape(WINDOW_KEYS + block_index, kv_local * HEAD_SIZE),
            start_position,
            0,
        )
        return (dq_all, attn_all, key_gradient_total, value_gradient_total)

    start_state = (
        jnp.zeros((shard, q_local * HEAD_SIZE), jnp.float32),
        jnp.zeros((shard, q_local * HEAD_SIZE), jnp.bfloat16),
        jnp.zeros((WINDOW_KEYS + shard, kv_local * HEAD_SIZE), jnp.float32),
        jnp.zeros((WINDOW_KEYS + shard, kv_local * HEAD_SIZE), jnp.float32),
    )
    dq_all, attn_all, key_gradient_total, value_gradient_total = lax.fori_loop(
        0, shard // block_index, step, start_state
    )
    back_keys, back_values = (
        shifted(key_gradient_total[:WINDOW_KEYS].astype(jnp.bfloat16), "context", -1).astype(
            jnp.float32
        ),
        shifted(value_gradient_total[:WINDOW_KEYS].astype(jnp.bfloat16), "context", -1).astype(
            jnp.float32
        ),
    )
    own_keys = key_gradient_total[WINDOW_KEYS:]
    own_values = value_gradient_total[WINDOW_KEYS:]
    key_grad = jnp.concatenate(
        [own_keys[: shard - WINDOW_KEYS], own_keys[shard - WINDOW_KEYS :] + back_keys], 0
    ).astype(jnp.bfloat16)
    value_grad = jnp.concatenate(
        [own_values[: shard - WINDOW_KEYS], own_values[shard - WINDOW_KEYS :] + back_values], 0
    ).astype(jnp.bfloat16)
    query_grad = dq_all.astype(jnp.bfloat16)
    weight_grad = lax.psum_scatter(
        lax.dot_general(
            grad_full, attn_all, (((0,), (0,)), ((), ())), preferred_element_type=jnp.float32
        ),
        "context",
        scatter_dimension=0,
        tiled=True,
    ).astype(jnp.bfloat16)
    return (query_grad, key_grad, value_grad, weight_grad)


def solution(mesh):
    return jax.shard_map(
        shards,
        mesh=mesh,
        in_specs=(
            P("context", "mp"),
            P("context", "mp"),
            P("context", "mp"),
            P(("context", "mp"), None),
            P(None, "mp"),
        ),
        out_specs=(P("context", "mp"), P("context", "mp"), P("context", "mp"), P("context", "mp")),
        check_vma=False,
    )
```

profile of v0, /device:TPU:1, one launch (start us, length us, event | category | flops | bytes accessed | tf_op | source)
XLA Modules:
  0.0 472.2 jit_solution(9497821260364624964)
XLA Ops:
  8.0 5.2 %collective-permute-start = (bf16[1024,128]{1,0:T(8,128)(2,1)}, bf16[1024,128]{1,0:T(8,128)(2,1)}, u32[]{:S(2)}, u32[]{:S(2)}) collective-permute-start(bf16[1024,128]{1,0:T(8,128)(2,1)} %param.8), channel_id=1, source_target_pairs={{0,8},{8,16},{16,24},{24,32},{32,40},{40,48},{48,56},{56,64},{64,7... | collective-permute-start | bytes 786440 | tf_op jit(solution)/shard_map/ppermute | solution.py:17
  13.2 2.9 collective-permute-start.1
  18.7 4.7 collective-permute-done.1
  24.9 52.5 %all-gather.2.cloned.1.call-done = bf16[1024,5376]{1,0:T(8,128)(2,1)} async-done(((bf16[128,5376]{1,0:T(8,128)(2,1)}), bf16[1024,5376]{1,0:T(8,128)(2,1)}) %all-gather.2.cloned.1.call-update) | async-done | bytes 11010064 | tf_op jit(solution)/shard_map/all_gather | solution.py:68
  77.4 7.9 %convolution_convert_fusion.1 = bf16[1024,256]{1,0:T(8,128)(2,1)} fusion(bf16[1024,5376]{1,0:T(8,128)(2,1)} %all-gather.2.cloned.1.call-done, bf16[5376,256]{1,0:T(8,128)(2,1)S(1)} %copy-done), kind=kOutput, calls=%fused_computation.47 | convolution fusion | flops 2818834432 | bytes 14286848 | tf_op jit(solution)/shard_map/dot_general | solution.py:69
  89.0 136.3 %while.19 = (s32[]{:T(128)}, bf16[1024,256]{1,0:T(8,128)(2,1)}, bf16[1024,256]{0,1:T(8,128)(2,1)}, f32[1536,128]{1,0:T(8,128)}, f32[1536,128]{1,0:T(8,128)}, /*i...) while((s32[]{:T(128)}, bf16[1024,256]{1,0:T(8,128)(2,1)}, ...), condition=%wide.region_4.5_spmd, body=%wide.region_0.4_spmd.sunk | while | flops 610795776 | bytes 35936128 | solution.py:128
  95.9 2.0 fusion.71
  97.9 3.1 fusion.72
  103.7 2.4 fusion.75
  111.6 2.2 fusion.74
  113.9 2.0 copy.89
  115.8 2.0 constant_dynamic-update-slice_fusion.9
  132.0 3.1 fusion.72
  137.7 2.4 fusion.75
  145.7 2.2 fusion.74
  147.9 2.0 copy.89
  149.9 2.0 constant_dynamic-update-slice_fusion.9
  166.0 3.1 fusion.72
  171.8 2.4 fusion.75
  179.8 2.2 fusion.74
  182.0 2.0 copy.89
  184.0 2.0 constant_dynamic-update-slice_fusion.9
  200.1 3.1 fusion.72
  205.8 2.4 fusion.75
  213.8 2.2 fusion.74
  216.0 2.0 copy.89
  218.0 2.1 constant_dynamic-update-slice_fusion.9
  225.2 9.7 %convolution_bitcast_fusion.2 = f32[5376,256]{0,1:T(8,128)} fusion(bf16[1024,256]{0,1:T(8,128)(2,1)} %get-tuple-element.179, bf16[1024,5376]{1,0:T(8,128)(2,1)} %all-gather.2.cloned.1.call-done), kind=kOutput, calls=%fused_computation.46 | convolution fusion | flops 2818572288 | bytes 17039360 | tf_op jit(solution)/shard_map/dot_general | solution.py:149
  234.9 6.1 %copy.66 = f32[5376,256]{1,0:T(8,128)} copy(f32[5376,256]{0,1:T(8,128)} %convolution_bitcast_fusion.2) | data formatting | bytes 11010048
  244.9 4.1 collective-permute-done.3
  249.8 2.1 collective-permute-done.2
  252.6 210.9 %reduce-scatter.4.cloned.1.call-done = f32[168,256]{1,0:T(8,128)} async-done(((f32[5376,256]{1,0:T(8,128)}), f32[168,256]{1,0:T(8,128)}) %reduce-scatter.4.cloned.1.call-update) | async-done | bytes 172048
  (146 shorter events, 102.8 us)
Async XLA Ops:
  7.2 70.3 %copy-start = (bf16[5376,256]{1,0:T(8,128)(2,1)S(1)}, bf16[5376,256]{1,0:T(8,128)(2,1)}, u32[]{:S(2)}) copy-start(bf16[5376,256]{1,0:T(8,128)(2,1)} %param.11) | copy-start | bytes 8257540
  7.2 16.2 %copy-start.7 = (bf16[1024,128]{1,0:T(8,128)(2,1)S(1)}, bf16[1024,128]{1,0:T(8,128)(2,1)}, u32[]{:S(2)}) copy-start(bf16[1024,128]{1,0:T(8,128)(2,1)} %param.8) | copy-start | bytes 786436
  7.2 17.0 %copy-start.8 = (bf16[1024,128]{1,0:T(8,128)(2,1)S(1)}, bf16[1024,128]{1,0:T(8,128)(2,1)}, u32[]{:S(2)}) copy-start(bf16[1024,128]{1,0:T(8,128)(2,1)} %param.9) | copy-start | bytes 786436
  7.2 70.2 %all-gather.2.cloned.1.call-start = ((), (), s32[]{:S(2)}) async-start(), calls=%async_computation.1 | async-start | bytes 12386304 | tf_op jit(solution)/shard_map/all_gather | solution.py:68
  7.9 455.6 %reduce-scatter.4.cloned.1.call-start = ((), (), s32[]{:S(2)}) async-start(), calls=%async_computation.2 | async-start | bytes 5677056
  8.0 9.8 %collective-permute-start = (bf16[1024,128]{1,0:T(8,128)(2,1)}, bf16[1024,128]{1,0:T(8,128)(2,1)}, u32[]{:S(2)}, u32[]{:S(2)}) collective-permute-start(bf16[1024,128]{1,0:T(8,128)(2,1)} %param.8), channel_id=1, source_target_pairs={{0,8},{8,16},{16,24},{24,32},{32,40},{40,48},{48,56},{56,64},{64,7... | collective-permute-start | bytes 786440 | tf_op jit(solution)/shard_map/ppermute | solution.py:17
  13.2 10.2 %collective-permute-start.1 = (bf16[1024,128]{1,0:T(8,128)(2,1)}, bf16[1024,128]{1,0:T(8,128)(2,1)S(1)}, u32[]{:S(2)}, u32[]{:S(2)}) collective-permute-start(bf16[1024,128]{1,0:T(8,128)(2,1)} %param.9), channel_id=1, source_target_pairs={{0,8},{8,16},{16,24},{24,32},{32,40},{40,48},{48,56},{56,64},{64,7... | collective-permute-start | bytes 786440 | tf_op jit(solution)/shard_map/ppermute | solution.py:17
  90.0 1.6 copy-start.3
  91.5 1.2 copy-start.1
  97.9 3.1 copy-start.4
  113.8 4.0 copy-start.2
  124.0 1.6 copy-start.3
  125.6 1.2 copy-start.1
  132.0 3.1 copy-start.4
  147.9 4.0 copy-start.2
  158.1 1.6 copy-start.3
  159.7 1.2 copy-start.1
  166.0 3.1 copy-start.4
  182.0 4.0 copy-start.2
  192.2 1.6 copy-start.3
  193.7 1.2 copy-start.1
  200.1 3.1 copy-start.4
  216.0 4.1 copy-start.2
  241.1 1.1 copy-start.6
  241.1 2.5 copy-start.5
  242.3 6.8 %collective-permute-start.3 = (bf16[512,128]{1,0:T(8,128)(2,1)S(1)}, bf16[512,128]{1,0:T(8,128)(2,1)S(1)}, u32[]{:S(2)}, u32[]{:S(2)}) collective-permute-start(bf16[512,128]{1,0:T(8,128)(2,1)S(1)} %get-tuple-element.249), channel_id=1, source_target_pairs={{8,0},{16,8},{24,16},{32,24},{40,32},{48,40},{56,48},{64,56},{72,6... | collective-permute-start | bytes 393224 | tf_op jit(solution)/shard_map/ppermute | solution.py:17
  243.6 8.2 %collective-permute-start.2 = (bf16[512,128]{1,0:T(8,128)(2,1)S(1)}, bf16[512,128]{1,0:T(8,128)(2,1)S(1)}, u32[]{:S(2)}, u32[]{:S(2)}) collective-permute-start(bf16[512,128]{1,0:T(8,128)(2,1)S(1)} %get-tuple-element.251), channel_id=1, source_target_pairs={{8,0},{16,8},{24,16},{32,24},{40,32},{48,40},{56,48},{64,56},{72,6... | collective-permute-start | bytes 393224 | tf_op jit(solution)/shard_map/ppermute | solution.py:17
Sparse Core Ops, SparseCore 0:
  9.9 67.5 all-gather.1
  241.2 222.2 reduce-scatter.3
where the time goes:
time: 477 us; the launch traced here: 472 us
  waiting for transfers between devices  277 us (58%)
  local copies, waits for them, and re-layouts  95.5 us (20%)
  matrix products  68.8 us (14%)
  between operations  14.2 us (3%)
  starting transfers between devices  10.7 us (2%)
  other arithmetic  5.89 us (1%)
    unnamed x3, waiting for transfers between devices  212 us
    all_gather x1, waiting for transfers between devices, shards(): grad_full = lax.all_gather(out_grad, 'mp', axis=0, tiled=True)  52.5 us
    dynamic_update_slice x8, local copies, waits for them, and re-layouts, step(): lax.dynamic_update_slice_in_dim(value_gradient_total, earlier_values + va...  16.1 us
    dynamic_slice x8, local copies, waits for them, and re-layouts, step(): lax.dynamic_slice_in_dim(value_gradient_total, start_position, WINDOW_KEY...  14.7 us
    dynamic_slice x8, local copies, waits for them, and re-layouts, step(): lax.dynamic_slice_in_dim(output_gradient, start_position, block_index, 0)  12.9 us
    ppermute x4, waiting for transfers between devices, shifted(): return lax.ppermute(x, axis, pairs)  12.6 us
    dot_general x4, matrix products, band_grads(): jnp.einsum('qhgd,khd->hgqk', output_grad_rows, value_rows_block, preferre...  12.2 us
    dynamic_slice x8, local copies, waits for them, and re-layouts, step(): lax.dynamic_slice_in_dim(key_gradient_total, start_position, WINDOW_KEYS...  10.7 us
  transfers between devices with their start and end apart: 6, of which 6 were waited for; matrix products, arithmetic and copies ran while one was open for 1% of the time, Pallas kernels for 0%

commit v1 on v0

v1 whole, which is shorter than its diff:
```python
import jax
import jax.numpy as jnp
from jax import lax
from jax.experimental import pallas as pl
from jax.experimental.pallas import tpu as pltpu
from jax.sharding import PartitionSpec as P

MESH = pl.DeviceIdType.MESH
F32 = jnp.float32
BF16 = jnp.bfloat16

SCALE = 168.0 ** (-0.5)
LOG2E = 1.4426950408889634
NEG = -1e30

SHARD = 1024
HALO = 512
ROWS = 128
SPAN = HALO + ROWS
D = 5376
XS, ZS, YS = 4, 8, 4
BLOCK = D // XS
PIECE = BLOCK // ZS
WIDE = 1408
UNIT = (1408, 1280, 1408, 1280)


def nt(a, b):
    return lax.dot_general(a, b, (((1,), (1,)), ((), ())), preferred_element_type=F32)


def nn(a, b):
    return jnp.dot(a, b, preferred_element_type=F32)


def flipped(a):
    return jnp.transpose(a.astype(F32), (1, 0)).astype(a.dtype)


def kernel(
    q_hbm, k_hbm, v_hbm, g_hbm, w_hbm, dq_hbm, dk_hbm, dv_hbm, dw_hbm,
    q, kf, vf, kt, vt, g, w, prob, at, do, dka, dva, wt, own,
    xs, ha, hb, r1, r2, zs, zr, bs, br, dqv, dkv, dvv, dwv,
    lsem, osem, ag_s, ag_r, halo_s, halo_r, x_s, x_r, z_s, z_r, back_s, back_r,
):
    c = lax.axis_index("context")
    m = lax.axis_index("mp")
    x, z = c // ZS, c % ZS
    y, core = m // 2, m % 2
    up = ((y + 1) % YS) * 2 + core
    down = ((y + YS - 1) % YS) * 2 + core
    far = ((y + 2) % YS) * 2 + core
    sib = y * 2 + (1 - core)
    x1 = x + 1 - 2 * (x % 2)
    x2 = (x + 2) % XS
    x3 = XS - 1 - x
    right = (c + 1) % (XS * ZS)
    left = (c + XS * ZS - 1) % (XS * ZS)

    local = [
        pltpu.make_async_copy(k_hbm, kf.at[pl.ds(HALO, SHARD)], lsem.at[0]),
        pltpu.make_async_copy(v_hbm, vf.at[pl.ds(HALO, SHARD)], lsem.at[1]),
        pltpu.make_async_copy(q_hbm, q, lsem.at[2]),
        pltpu.make_async_copy(g_hbm, g.at[pl.ds(pl.multiple_of(m * ROWS, ROWS), ROWS)], lsem.at[3]),
        pltpu.make_async_copy(w_hbm, w, lsem.at[4]),
    ]
    for copy in local:
        copy.start()

    peers = [(c, up), (c, down), (c, sib), (x1 * ZS + z, m), (x3 * ZS + z, m), (right, m), (left, m)]
    peers += [(x * ZS + (z + d) % ZS, m) for d in range(1, ZS)]
    barrier = pltpu.get_barrier_semaphore()
    for peer in peers:
        pl.semaphore_signal(barrier, inc=1, device_id=peer, device_id_type=MESH)
    pl.semaphore_wait(barrier, len(peers))

    def remote(src, dst, s, r, peer):
        return pltpu.make_async_remote_copy(
            src_ref=src, dst_ref=dst, send_sem=s, recv_sem=r, device_id=peer, device_id_type=MESH
        )

    blocks = (x2, x3, x1, x)

    def wide_start(b):
        return pl.multiple_of((21 * (b // 2) + 10 * (b % 2)) * 128, 128)

    def unit_start(step):
        b = blocks[step]
        if step % 2 == 0:
            return wide_start(b)
        return pl.multiple_of((21 * (b // 2) + 11 * (b % 2)) * 128, 128)

    def rows_of(shard, first, count):
        return pl.ds(pl.multiple_of(shard * ROWS + first, 64), count)

    def ag_copy(step, kind):
        cols = pl.ds(unit_start(step), UNIT[step])
        target = (c, (up, down, up, down, sib, sib, sib, sib, sib)[kind])
        shard, first, count = (
            (m, 0, 128), (m, 0, 128), (down, 0, 64), (up, 64, 64), (m, 0, 128),
            (down, 0, 128), (up, 0, 128), (far, 0, 64), (far, 64, 64),
        )[kind]
        dst = g.at[rows_of(shard, first, count), cols]
        src = g_hbm.at[:, cols] if kind in (0, 1, 4) else dst
        return remote(src, dst, ag_s.at[step, kind], ag_r.at[step, kind], target)

    ag = [[ag_copy(step, kind) for kind in range(9)] for step in range(4)]

    def start(step, *kinds):
        for kind in kinds:
            ag[step][kind].start()

    def arrive(step, *kinds):
        for kind in kinds:
            ag[step][kind].wait_recv()

    def service_near(step):
        arrive(step, 0)
        start(step, 2, 5)
        arrive(step, 1)
        start(step, 3, 6)

    def service_far(step):
        arrive(step, 2)
        start(step, 7)
        arrive(step, 3)
        start(step, 8)

    halo = [
        remote(k_hbm.at[pl.ds(SHARD - HALO, HALO)], kf.at[pl.ds(0, HALO)], halo_s.at[0], halo_r.at[0], (right, m)),
        remote(v_hbm.at[pl.ds(SHARD - HALO, HALO)], vf.at[pl.ds(0, HALO)], halo_s.at[1], halo_r.at[1], (right, m)),
    ]
    start(0, 0, 1)
    for copy in halo:
        copy.start()
    start(0, 4)
    start(1, 0, 1, 4)

    def keys_of(b):
        return pl.ds(pl.multiple_of(b * ROWS, ROWS), SPAN)

    def rows_at(b):
        return pl.ds(pl.multiple_of(b * ROWS, ROWS), ROWS)

    def query_rows(b):
        block = q[rows_at(b), :]
        return jnp.concatenate([block[:, :128], block[:, 128:]], 0)

    key_at = lax.broadcasted_iota(jnp.int32, (ROWS, 2 * ROWS), 0)
    query_at = lax.broadcasted_iota(jnp.int32, (ROWS, 2 * ROWS), 1) % ROWS

    def forward(b, with_halo):
        s = nt(kf[keys_of(b), :], query_rows(b)) * (SCALE * LOG2E)
        s = jnp.concatenate(
            [
                jnp.where(key_at > query_at, s[:ROWS], NEG),
                s[ROWS:HALO],
                jnp.where(key_at <= query_at, s[HALO:], NEG),
            ],
            0,
        )
        if with_halo:
            missing = jnp.where(c == 0, HALO - b * ROWS, 0)
            place = lax.broadcasted_iota(jnp.int32, (SPAN, 2 * ROWS), 0)
            s = jnp.where(place >= missing, s, NEG)
        e = jnp.exp2(s - jnp.max(s, axis=0, keepdims=True))
        p = e * (1.0 / jnp.sum(e, axis=0, keepdims=True))
        prob[b] = p
        a = nn(vt[:, keys_of(b)], p.astype(BF16)).astype(BF16)
        at[:128, rows_at(b)] = a[:, :128]
        at[128:, rows_at(b)] = a[:, 128:]

    for i in (0, 1, 2):
        local[i].wait()
    kt[:, HALO:] = flipped(kf[HALO:, :])
    vt[:, HALO:] = flipped(vf[HALO:, :])

    @pl.loop(4, 8)
    def _(b):
        forward(b, False)

    service_near(0)
    start(2, 0, 1, 4)

    for copy in halo:
        copy.wait_recv()
    kt[:, :HALO] = flipped(kf[:HALO, :])
    vt[:, :HALO] = flipped(vf[:HALO, :])

    @pl.loop(0, 4)
    def _(b):
        forward(b, True)

    service_far(0)
    for i in (3, 4):
        local[i].wait()

    def weight_block(step):
        first = wide_start(blocks[step])
        for o in range(0, WIDE, 256):
            n = min(256, WIDE - o)
            part = nn(at[...], g[:, pl.ds(pl.multiple_of(first + o, 128), n)])
            wt[o : o + n, :] = jnp.transpose(part, (1, 0))

    def piece(step, i):
        b = blocks[step]
        return wt[pl.ds(pl.multiple_of((b % 2) * 64 + i * PIECE, 8), PIECE), :]

    def dout_part(step):
        cols = pl.ds(unit_start(step), UNIT[step])

        @pl.loop(0, 4)
        def _(t):
            rows = pl.ds(pl.multiple_of(t * 256, 256), 256)
            part = nn(g[rows, cols], w[cols, :])
            if step == 0:
                do[rows, :] = part
            else:
                do[rows, :] += part

    x_copies = [
        remote(xs.at[0, pl.ds(0, 4)], ha, x_s.at[0], x_r.at[0], (x1 * ZS + z, m)),
        remote(xs.at[0, pl.ds(4, 4)], hb, x_s.at[1], x_r.at[1], (x3 * ZS + z, m)),
        remote(xs.at[1], r1, x_s.at[2], x_r.at[2], (x3 * ZS + z, m)),
        remote(xs.at[2], r2, x_s.at[3], x_r.at[3], (x1 * ZS + z, m)),
    ]

    service_near(1)
    start(3, 0, 1, 4)
    arrive(0, 4, 5, 6, 7, 8)
    weight_block(0)
    for i in range(ZS):
        xs[0, i] = piece(0, i).astype(BF16)
    x_copies[0].start()
    x_copies[1].start()
    dout_part(0)

    service_far(1)
    service_near(2)
    arrive(1, 4, 5, 6, 7, 8)
    weight_block(1)
    x_copies[0].wait_recv()
    for i in range(ZS):
        t = piece(1, i)
        if i < 4:
            t = t + ha[i].astype(F32)
        xs[1, i] = t.astype(BF16)
    x_copies[2].start()
    dout_part(1)

    service_far(2)
    service_near(3)
    arrive(2, 4, 5, 6, 7, 8)
    weight_block(2)
    x_copies[1].wait_recv()
    for i in range(ZS):
        t = piece(2, i)
        if i >= 4:
            t = t + hb[i - 4].astype(F32)
        xs[2, i] = t.astype(BF16)
    x_copies[3].start()
    dout_part(2)

    service_far(3)
    arrive(3, 4, 5, 6, 7, 8)
    weight_block(3)
    x_copies[2].wait_recv()
    x_copies[3].wait_recv()
    z_copies = []
    for d in (4, 3, 5, 2, 6, 1, 7):
        to = (z + d) % ZS
        zs[to] = (piece(3, to) + r1[to].astype(F32) + r2[to].astype(F32)).astype(BF16)
        copy = remote(zs.at[to], zr.at[d - 1], z_s.at[d - 1], z_r.at[d - 1], (x * ZS + to, m))
        copy.start()
        z_copies.append(copy)
    own[...] = piece(3, z) + r1[z].astype(F32) + r2[z].astype(F32)
    dout_part(3)

    def backward(b):
        qb = query_rows(b)
        block = do[rows_at(b), :].astype(BF16)
        db = jnp.concatenate([block[:, :128], block[:, 128:]], 0)
        dt = jnp.transpose(db.astype(F32), (1, 0))
        a = jnp.concatenate([at[:128, rows_at(b)], at[128:, rows_at(b)]], 1).astype(F32)
        delta = jnp.sum(dt * a, axis=0, keepdims=True)
        p = prob[b]
        ds = (p * (nt(vf[keys_of(b), :], db) - delta)).astype(BF16)
        dqt = nn(kt[:, keys_of(b)], ds) * SCALE
        dqv[rows_at(b), :128] = jnp.transpose(dqt[:, :128], (1, 0)).astype(BF16)
        dqv[rows_at(b), 128:] = jnp.transpose(dqt[:, 128:], (1, 0)).astype(BF16)
        dka[keys_of(b), :] += nn(ds, qb)
        dva[keys_of(b), :] += nn(p.astype(BF16), db)

    dka[...] = jnp.zeros_like(dka)
    dva[...] = jnp.zeros_like(dva)

    @pl.loop(0, 4)
    def _(b):
        backward(b)

    bs[0] = (dka[:HALO, :] * SCALE).astype(BF16)
    bs[1] = dva[:HALO, :].astype(BF16)
    back = remote(bs, br, back_s, back_r, (left, m))
    back.start()

    @pl.loop(4, 8)
    def _(b):
        backward(b)

    outs = [pltpu.make_async_copy(dqv, dq_hbm, osem.at[0])]
    outs[0].start()
    total = own[...]
    for copy, d in zip(z_copies, (4, 3, 5, 2, 6, 1, 7)):
        copy.wait_recv()
        total = total + zr[d - 1].astype(F32)
    dwv[...] = total.astype(BF16)
    outs.append(pltpu.make_async_copy(dwv, dw_hbm, osem.at[1]))
    outs[1].start()
    dkv[:HALO, :] = (dka[HALO:SHARD, :] * SCALE).astype(BF16)
    dvv[:HALO, :] = dva[HALO:SHARD, :].astype(BF16)
    back.wait_recv()
    dkv[HALO:, :] = (dka[SHARD:, :] * SCALE + br[0].astype(F32)).astype(BF16)
    dvv[HALO:, :] = (dva[SHARD:, :] + br[1].astype(F32)).astype(BF16)
    outs.append(pltpu.make_async_copy(dkv, dk_hbm, osem.at[2]))
    outs.append(pltpu.make_async_copy(dvv, dv_hbm, osem.at[3]))
    outs[2].start()
    outs[3].start()
    for step in range(4):
        for kind in range(9):
            ag[step][kind].wait_send()
    for copy in halo + x_copies + z_copies + [back]:
        copy.wait_send()
    for copy in outs:
        copy.wait()


def shards(queries, keys, values, out_grad, out_weight):
    vmem = pltpu.VMEM
    dma = pltpu.SemaphoreType.DMA
    scratch = [
        vmem((SHARD, 256), BF16),
        vmem((HALO + SHARD, 128), BF16),
        vmem((HALO + SHARD, 128), BF16),
        vmem((128, HALO + SHARD), BF16),
        vmem((128, HALO + SHARD), BF16),
        vmem((SHARD, D), BF16),
        vmem((D, 256), BF16),
        vmem((8, SPAN, 256), F32),
        vmem((256, SHARD), BF16),
        vmem((SHARD, 256), F32),
        vmem((HALO + SHARD, 128), F32),
        vmem((HALO + SHARD, 128), F32),
        vmem((WIDE, 256), F32),
        vmem((PIECE, 256), F32),
        vmem((3, ZS, PIECE, 256), BF16),
        vmem((4, PIECE, 256), BF16),
        vmem((4, PIECE, 256), BF16),
        vmem((ZS, PIECE, 256), BF16),
        vmem((ZS, PIECE, 256), BF16),
        vmem((ZS, PIECE, 256), BF16),
        vmem((ZS - 1, PIECE, 256), BF16),
        vmem((2, HALO, 128), BF16),
        vmem((2, HALO, 128), BF16),
        vmem((SHARD, 256), BF16),
        vmem((SHARD, 128), BF16),
        vmem((SHARD, 128), BF16),
        vmem((PIECE, 256), BF16),
        dma((5,)), dma((4,)), dma((4, 9)), dma((4, 9)), dma((2,)), dma((2,)),
        dma((4,)), dma((4,)), dma((7,)), dma((7,)), dma, dma,
    ]
    hbm = pl.BlockSpec(memory_space=pl.ANY)
    return pl.pallas_call(
        kernel,
        out_shape=(
            jax.ShapeDtypeStruct((SHARD, 256), BF16),
            jax.ShapeDtypeStruct((SHARD, 128), BF16),
            jax.ShapeDtypeStruct((SHARD, 128), BF16),
            jax.ShapeDtypeStruct((PIECE, 256), BF16),
        ),
        in_specs=[hbm] * 5,
        out_specs=(hbm,) * 4,
        scratch_shapes=scratch,
        compiler_params=pltpu.CompilerParams(
            collective_id=0, has_side_effects=True, vmem_limit_bytes=56 * 1024 * 1024
        ),
        name="attention_grads",
    )(queries, keys, values, out_grad, out_weight)


def solution(mesh):
    return jax.shard_map(
        shards,
        mesh=mesh,
        in_specs=(
            P("context", "mp"),
            P("context", "mp"),
            P("context", "mp"),
            P(("context", "mp"), None),
            P(None, "mp"),
        ),
        out_specs=(P("context", "mp"), P("context", "mp"), P("context", "mp"), P("context", "mp")),
        check_vma=False,
    )
```

time: 477 us -> 104 us (0.22)
  waiting for transfers between devices: 277 us -> 0 us
  Pallas kernels: 0 us -> 96.1 us
  local copies, waits for them, and re-layouts: 95.5 us -> 6.74 us
  matrix products: 68.8 us -> 0 us
  between operations: 14.2 us -> 0.64 us
  starting transfers between devices: 10.7 us -> 0 us
  other arithmetic: 5.89 us -> 0 us
    unnamed x3 -> x0, waiting for transfers between devices: 212 us -> none
    pallas_call x0 -> x1, Pallas kernels: none -> 96.1 us  [shards(): pl.pallas_call(kernel, out_shape=(jax.ShapeDtypeStruct((SHARD, 256), BF16...]
    dot_general x26 -> x0, matrix products: 68.8 us -> none  [the longest x4 12.2 us: band_grads(): jnp.einsum('qhgd,khd->hgqk', output_grad_rows, value_rows_block, preferre...]
    all_gather x1 -> x0, waiting for transfers between devices: 52.5 us -> none  [shards(): grad_full = lax.all_gather(out_grad, 'mp', axis=0, tiled=True)]
    dynamic_slice x32 -> x0, local copies, waits for them, and re-layouts: 42.4 us -> none  [the longest x8 14.7 us: step(): lax.dynamic_slice_in_dim(value_gradient_total, start_position, WINDOW_KEY...]
    dynamic_update_slice x24 -> x0, local copies, waits for them, and re-layouts: 36.8 us -> none  [the longest x8 16.1 us: step(): lax.dynamic_update_slice_in_dim(value_gradient_total, earlier_values + va...]
    ppermute x4 -> x0, waiting for transfers between devices: 12.6 us -> none  [shifted(): return lax.ppermute(x, axis, pairs)]
    ppermute x4 -> x0, starting transfers between devices: 10.7 us -> none  [shifted(): return lax.ppermute(x, axis, pairs)]
  transfers between devices with their start and end apart: 6 -> 0, of which waited for: 6 -> 0; matrix products, arithmetic and copies ran while one was open for 1% -> 0% of each run, Pallas kernels for 0% -> 0%
where the time goes in v1:
time: 104 us; the launch traced here: 103 us
  Pallas kernels  96.1 us (92%)
  local copies, waits for them, and re-layouts  6.74 us (6%)
    pallas_call x1, Pallas kernels, shards(): pl.pallas_call(kernel, out_shape=(jax.ShapeDtypeStruct((SHARD, 256), BF16...  96.1 us
    unnamed x4, local copies, waits for them, and re-layouts  6.74 us

profile of v1, /device:TPU:1, one launch (start us, length us, event | category | flops | bytes accessed | tf_op | source)
XLA Modules:
  0.0 103.4 jit_solution(5095518607611112673)
XLA Ops:
  0.6 96.1 %attention_grads.1 = (bf16[1024,256]{1,0:T(8,128)(2,1)}, bf16[1024,128]{1,0:T(8,128)(2,1)}, bf16[1024,128]{1,0:T(8,128)(2,1)}, bf16[168,256]{1,0:T(8,128)(2,1)}) custom-call(bf16[1024,256]{1,0:T(8,128)(2,1)} %q_hbm.1, bf16[1024,128]{1,0:T(8,128)(2,1)} %k_hbm.1, bf16[1024,128]{1,0:T(8,128)(2,1)} %v_hbm.1, bf16[128,5376]{1,0:T(8,128)(2,1)} %g_hbm.1, ...), custom_call_target="tpu_custom_call" | custom-call | tf_op jit(solution)/shard_map/attention_grads/pallas_call | solution.py:372
  96.7 1.9 %copy.13 = bf16[1024,256]{1,0:T(8,128)(2,1)} copy(bf16[1024,256]{1,0:T(8,128)(2,1)} %get-tuple-element.8) | data formatting | bytes 1048576
  98.6 1.7 %copy.14 = bf16[1024,128]{1,0:T(8,128)(2,1)} copy(bf16[1024,128]{1,0:T(8,128)(2,1)} %get-tuple-element.9) | data formatting | bytes 524288
  100.2 1.7 %copy.15 = bf16[1024,128]{1,0:T(8,128)(2,1)} copy(bf16[1024,128]{1,0:T(8,128)(2,1)} %get-tuple-element.10) | data formatting | bytes 524288
  101.9 1.5 %copy.16 = bf16[168,256]{1,0:T(8,128)(2,1)} copy(bf16[168,256]{1,0:T(8,128)(2,1)} %get-tuple-element.11) | data formatting | bytes 172032

commit v2 on v1

v2 whole, which is shorter than its diff:
```python
import jax
import jax.numpy as jnp
from jax import lax
from jax.experimental import pallas as pl
from jax.experimental.pallas import tpu as pltpu
from jax.sharding import PartitionSpec as P

MESH = pl.DeviceIdType.MESH
F32 = jnp.float32
BF16 = jnp.bfloat16

SCALE = 168.0 ** (-0.5)
LOG2E = 1.4426950408889634
NEG = -1e30

SHARD = 1024
HALO = 512
ROWS = 128
SPAN = HALO + ROWS
D = 5376
XS, ZS, YS = 4, 8, 4
PIECE = D // (XS * ZS)
BLOCK = XS * PIECE
WIDE = 768
STEPS = ZS
ENDS = tuple(-(-BLOCK * (s + 1) // 128) * 128 for s in range(STEPS))
BEGINS = (0,) + ENDS[:-1]
AHEAD = 2


def nt(a, b):
    return lax.dot_general(a, b, (((1,), (1,)), ((), ())), preferred_element_type=F32)


def nn(a, b):
    return jnp.dot(a, b, preferred_element_type=F32)


def flipped(a):
    return jnp.transpose(a.astype(F32), (1, 0)).astype(a.dtype)


def kernel(
    q_hbm, k_hbm, v_hbm, g_hbm, w_hbm, dq_hbm, dk_hbm, dv_hbm, dw_hbm,
    q, kf, vf, kt, vt, gown, g, wp, wf, wb, prob, at, do, dka, dva, wt,
    as_, bs_, ar, br, sx, fs, fr, hs, hr, dqv, dkv, dvv, dwv,
    lsem, osem, ag_s, ag_r, halo_s, halo_r, za_s, za_r, zb_s, zb_r, x_s, x_r, back_s, back_r,
):
    c = lax.axis_index("context")
    m = lax.axis_index("mp")
    x, z = c // ZS, c % ZS
    y, core = m // 2, m % 2
    up = ((y + 1) % YS) * 2 + core
    down = ((y + YS - 1) % YS) * 2 + core
    far = ((y + 2) % YS) * 2 + core
    sib = y * 2 + (1 - core)
    right = (c + 1) % (XS * ZS)
    left = (c + XS * ZS - 1) % (XS * ZS)
    above = x * ZS + (z + 1) % ZS
    below = x * ZS + (z + ZS - 1) % ZS

    def target_z(z, step, i):
        return (z + ZS - 1 - step) % ZS if i < 2 else (z + 1 + step) % ZS

    local = [
        pltpu.make_async_copy(g_hbm, gown, lsem.at[0]),
        pltpu.make_async_copy(k_hbm, kf.at[pl.ds(HALO, SHARD)], lsem.at[1]),
        pltpu.make_async_copy(v_hbm, vf.at[pl.ds(HALO, SHARD)], lsem.at[2]),
        pltpu.make_async_copy(q_hbm, q, lsem.at[3]),
        pltpu.make_async_copy(w_hbm, wp, lsem.at[4]),
    ]
    for copy in local:
        copy.start()
    peers = [(c, up), (c, down), (c, sib), (above, m), (below, m), (right, m), (left, m)]
    peers += [(((x + e) % XS) * ZS + z, m) for e in range(1, XS)]
    barrier = pltpu.get_barrier_semaphore()
    for peer in peers:
        pl.semaphore_signal(barrier, inc=1, device_id=peer, device_id_type=MESH)
    def reorder(first, last):
        for zz in range(ZS):

            @pl.when(z == zz)
            def _():
                @pl.loop(0, ROWS // 16)
                def _(t):
                    rows = pl.ds(pl.multiple_of(t * 16, 16), 16)
                    out_rows = pl.ds(pl.multiple_of(m * ROWS + t * 16, 16), 16)
                    for tile in range(first // 128, last // 128):
                        parts = []
                        at_col = tile * 128
                        while at_col < tile * 128 + 128:
                            n, inside = at_col // PIECE, at_col % PIECE
                            count = min(PIECE - inside, tile * 128 + 128 - at_col)
                            step, i = n // XS, n % XS
                            begin = (i * ZS + target_z(zz, step, i)) * PIECE + inside
                            while count > 0:
                                part = min(count, 128 - begin % 128)
                                base = begin // 128 * 128
                                tile_in = gown[rows, base : base + 128].astype(F32)
                                parts.append(tile_in[:, begin % 128 : begin % 128 + part])
                                begin += part
                                at_col += part
                                count -= part
                        g[out_rows, tile * 128 : tile * 128 + 128] = (
                            parts[0] if len(parts) == 1 else jnp.concatenate(parts, 1)
                        ).astype(BF16)

    def remote(src, dst, s, r, peer):
        return pltpu.make_async_remote_copy(
            src_ref=src, dst_ref=dst, send_sem=s, recv_sem=r, device_id=peer, device_id_type=MESH
        )

    def ag_copy(step, kind):
        target = (c, (up, down, up, down, sib, sib, sib, sib, sib)[kind])
        shard, first, count = (
            (m, 0, 128), (m, 0, 128), (down, 0, 64), (up, 64, 64), (m, 0, 128),
            (down, 0, 128), (up, 0, 128), (far, 0, 64), (far, 64, 64),
        )[kind]
        rows = pl.ds(pl.multiple_of(shard * ROWS + first, 64), count)
        part = g.at[rows, pl.ds(BEGINS[step], ENDS[step] - BEGINS[step])]
        return remote(part, part, ag_s.at[step, kind], ag_r.at[step, kind], target)

    ag = [[ag_copy(step, kind) for kind in range(9)] for step in range(STEPS)]

    def start(step, *kinds):
        for kind in kinds:
            ag[step][kind].start()

    def arrive(step, *kinds):
        for kind in kinds:
            ag[step][kind].wait_recv()

    def service_near(step):
        arrive(step, 0)
        start(step, 2, 5)
        arrive(step, 1)
        start(step, 3, 6)
        if step + AHEAD < STEPS:
            start(step + AHEAD, 0, 1, 4)

    def service_far(step):
        arrive(step, 2)
        start(step, 7)
        arrive(step, 3)
        start(step, 8)

    halo = [
        remote(k_hbm.at[pl.ds(SHARD - HALO, HALO)], kf.at[pl.ds(0, HALO)], halo_s.at[0], halo_r.at[0], (right, m)),
        remote(v_hbm.at[pl.ds(SHARD - HALO, HALO)], vf.at[pl.ds(0, HALO)], halo_s.at[1], halo_r.at[1], (right, m)),
    ]
    local[0].wait()
    reorder(BEGINS[0], ENDS[0])
    pl.semaphore_wait(barrier, len(peers))
    start(0, 0, 1)
    for copy in halo:
        copy.start()
    start(0, 4)
    reorder(BEGINS[1], ENDS[1])
    start(1, 0, 1, 4)
    reorder(BEGINS[2], ENDS[STEPS - 1])

    def keys_of(b):
        return pl.ds(pl.multiple_of(b * ROWS, ROWS), SPAN)

    def rows_at(b):
        return pl.ds(pl.multiple_of(b * ROWS, ROWS), ROWS)

    def query_rows(b):
        block = q[rows_at(b), :]
        return jnp.concatenate([block[:, :128], block[:, 128:]], 0)

    key_at = lax.broadcasted_iota(jnp.int32, (ROWS, 2 * ROWS), 0)
    query_at = lax.broadcasted_iota(jnp.int32, (ROWS, 2 * ROWS), 1) % ROWS

    def forward(b, with_halo):
        s = nt(kf[keys_of(b), :], query_rows(b)) * (SCALE * LOG2E)
        s = jnp.concatenate(
            [
                jnp.where(key_at > query_at, s[:ROWS], NEG),
                s[ROWS:HALO],
                jnp.where(key_at <= query_at, s[HALO:], NEG),
            ],
            0,
        )
        if with_halo:
            missing = jnp.where(c == 0, HALO - b * ROWS, 0)
            place = lax.broadcasted_iota(jnp.int32, (SPAN, 2 * ROWS), 0)
            s = jnp.where(place >= missing, s, NEG)
        e = jnp.exp2(s - jnp.max(s, axis=0, keepdims=True))
        p = e * (1.0 / jnp.sum(e, axis=0, keepdims=True))
        prob[b] = p
        a = nn(vt[:, keys_of(b)], p.astype(BF16)).astype(BF16)
        at[:128, rows_at(b)] = a[:, :128]
        at[128:, rows_at(b)] = a[:, 128:]

    for i in (1, 2, 3):
        local[i].wait()
    kt[:, HALO:] = flipped(kf[HALO:, :])
    vt[:, HALO:] = flipped(vf[HALO:, :])

    @pl.loop(4, 8)
    def _(b):
        forward(b, False)

    service_near(0)
    for copy in halo:
        copy.wait_recv()
    kt[:, :HALO] = flipped(kf[:HALO, :])
    vt[:, :HALO] = flipped(vf[:HALO, :])

    @pl.loop(0, 4)
    def _(b):
        forward(b, True)

    service_far(0)
    service_near(1)
    local[4].wait()
    wf[...] = wp[...].astype(F32)

    @pl.loop(0, STEPS)
    def _(step):
        for half in (0, 2):
            two = []
            for i in (half, half + 1):
                p = i * ZS + target_z(z, step, i)
                two.append(wf[pl.ds(pl.multiple_of(p * PIECE, 8), PIECE), :])
            rows = pl.ds(pl.multiple_of(step * BLOCK + half * PIECE, 16), 2 * PIECE)
            wb[rows, :] = jnp.concatenate(two, 0).astype(BF16)

    def dout_part(step):
        cols = slice(BEGINS[step], ENDS[step])

        @pl.loop(0, 4)
        def _(t):
            rows = pl.ds(pl.multiple_of(t * 256, 256), 256)
            part = nn(g[rows, cols], wb[cols, :])
            if step == 0:
                do[rows, :] = part
            else:
                do[rows, :] += part

    z_copies = []

    def weight_part(step):
        first = step * BLOCK // 128 * 128
        for o in range(0, WIDE, 256):
            part = nn(at[...], g[:, first + o : first + o + 256])
            wt[o : o + 256, :] = jnp.transpose(part, (1, 0))
        if step > 0:
            for copy in z_copies[-2:]:
                copy.wait_recv()
        for i in range(XS):
            begin = step * BLOCK - first + i * PIECE
            t = wt[begin : begin + PIECE, :]
            if step > 0:
                t = t + (ar[step - 1, i] if i < 2 else br[step - 1, i - 2]).astype(F32)
            if step == STEPS - 1:
                sx[i] = t
                fs[i] = t.astype(BF16)
            elif i < 2:
                as_[step, i] = t.astype(BF16)
            else:
                bs_[step, i - 2] = t.astype(BF16)
        if step < STEPS - 1:
            z_copies.append(remote(as_.at[step], ar.at[step], za_s.at[step], za_r.at[step], (above, m)))
            z_copies.append(remote(bs_.at[step], br.at[step], zb_s.at[step], zb_r.at[step], (below, m)))
            for copy in z_copies[-2:]:
                copy.start()

    for step in range(STEPS):
        if step > 0:
            service_far(step)
        if 0 < step < STEPS - 1:
            service_near(step + 1)
        arrive(step, 4, 5, 6, 7, 8)
        weight_part(step)
        if step < STEPS - 1:
            dout_part(step)

    x_copies = []
    for e in (2, 1, 3):
        to = (x + e) % XS
        x_copies.append(remote(fs.at[to], fr.at[e - 1], x_s.at[e - 1], x_r.at[e - 1], (to * ZS + z, m)))
        x_copies[-1].start()
    dout_part(STEPS - 1)

    def backward(b):
        qb = query_rows(b)
        block = do[rows_at(b), :].astype(BF16)
        db = jnp.concatenate([block[:, :128], block[:, 128:]], 0)
        dt = jnp.transpose(db.astype(F32), (1, 0))
        a = jnp.concatenate([at[:128, rows_at(b)], at[128:, rows_at(b)]], 1).astype(F32)
        delta = jnp.sum(dt * a, axis=0, keepdims=True)
        p = prob[b]
        ds = (p * (nt(vf[keys_of(b), :], db) - delta)).astype(BF16)
        dqt = nn(kt[:, keys_of(b)], ds) * SCALE
        dqv[rows_at(b), :128] = jnp.transpose(dqt[:, :128], (1, 0)).astype(BF16)
        dqv[rows_at(b), 128:] = jnp.transpose(dqt[:, 128:], (1, 0)).astype(BF16)
        dka[keys_of(b), :] += nn(ds, qb)
        dva[keys_of(b), :] += nn(p.astype(BF16), db)

    dka[...] = jnp.zeros_like(dka)
    dva[...] = jnp.zeros_like(dva)

    def back(b):
        return remote(hs.at[b], hr.at[b], back_s.at[b], back_r.at[b], (left, m))

    @pl.loop(0, 4)
    def _(b):
        backward(b)
        hs[b, 0] = (dka[rows_at(b), :] * SCALE).astype(BF16)
        hs[b, 1] = dva[rows_at(b), :].astype(BF16)
        back(b).start()

    @pl.loop(4, 8)
    def _(b):
        backward(b)

    outs = [pltpu.make_async_copy(dqv, dq_hbm, osem.at[0])]
    outs[0].start()
    total = sx[x]
    for copy, e in zip(x_copies, (2, 1, 3)):
        copy.wait_recv()
        total = total + fr[e - 1].astype(F32)
    dwv[...] = total.astype(BF16)
    outs.append(pltpu.make_async_copy(dwv, dw_hbm, osem.at[1]))
    outs[1].start()
    dkv[:HALO, :] = (dka[HALO:SHARD, :] * SCALE).astype(BF16)
    dvv[:HALO, :] = dva[HALO:SHARD, :].astype(BF16)
    for b in range(4):
        back(b).wait_recv()
        rows = slice(HALO + b * ROWS, HALO + (b + 1) * ROWS)
        late = slice(SHARD + b * ROWS, SHARD + (b + 1) * ROWS)
        dkv[rows, :] = (dka[late, :] * SCALE + hr[b, 0].astype(F32)).astype(BF16)
        dvv[rows, :] = (dva[late, :] + hr[b, 1].astype(F32)).astype(BF16)
    outs.append(pltpu.make_async_copy(dkv, dk_hbm, osem.at[2]))
    outs.append(pltpu.make_async_copy(dvv, dv_hbm, osem.at[3]))
    outs[2].start()
    outs[3].start()
    for step in range(STEPS):
        for kind in range(9):
            ag[step][kind].wait_send()
    for copy in halo + z_copies + x_copies + [back(b) for b in range(4)]:
        copy.wait_send()
    for copy in outs:
        copy.wait()


def hand_on(*refs):
    ins, outs, held, sem = refs[:4], refs[4:8], refs[8:12], refs[12]
    first = [pltpu.make_async_copy(ins[i], held[i], sem.at[0, i]) for i in range(4)]
    second = [pltpu.make_async_copy(held[i], outs[i], sem.at[1, i]) for i in range(4)]
    for copy in first:
        copy.start()
    for i in (3, 1, 2, 0):
        first[i].wait()
        second[i].start()
    for copy in second:
        copy.wait()


def shards(queries, keys, values, out_grad, out_weight):
    vmem = pltpu.VMEM
    dma = pltpu.SemaphoreType.DMA
    scratch = [
        vmem((SHARD, 256), BF16),
        vmem((HALO + SHARD, 128), BF16),
        vmem((HALO + SHARD, 128), BF16),
        vmem((128, HALO + SHARD), BF16),
        vmem((128, HALO + SHARD), BF16),
        vmem((ROWS, D), BF16),
        vmem((SHARD, D), BF16),
        vmem((D, 256), BF16),
        vmem((D, 256), F32),
        vmem((D, 256), BF16),
        vmem((8, SPAN, 256), F32),
        vmem((256, SHARD), BF16),
        vmem((SHARD, 256), F32),
        vmem((HALO + SHARD, 128), F32),
        vmem((HALO + SHARD, 128), F32),
        vmem((WIDE, 256), F32),
        vmem((STEPS - 1, 2, PIECE, 256), BF16),
        vmem((STEPS - 1, 2, PIECE, 256), BF16),
        vmem((STEPS - 1, 2, PIECE, 256), BF16),
        vmem((STEPS - 1, 2, PIECE, 256), BF16),
        vmem((XS, PIECE, 256), F32),
        vmem((XS, PIECE, 256), BF16),
        vmem((XS - 1, PIECE, 256), BF16),
        vmem((4, 2, ROWS, 128), BF16),
        vmem((4, 2, ROWS, 128), BF16),
        vmem((SHARD, 256), BF16),
        vmem((SHARD, 128), BF16),
        vmem((SHARD, 128), BF16),
        vmem((PIECE, 256), BF16),
        dma((5,)), dma((4,)), dma((STEPS, 9)), dma((STEPS, 9)), dma((2,)), dma((2,)),
        dma((7,)), dma((7,)), dma((7,)), dma((7,)), dma((3,)), dma((3,)), dma((4,)), dma((4,)),
    ]
    hbm = pl.BlockSpec(memory_space=pl.ANY)
    shapes = (
        jax.ShapeDtypeStruct((SHARD, 256), BF16),
        jax.ShapeDtypeStruct((SHARD, 128), BF16),
        jax.ShapeDtypeStruct((SHARD, 128), BF16),
        jax.ShapeDtypeStruct((PIECE, 256), BF16),
    )
    grads = pl.pallas_call(
        kernel,
        out_shape=shapes,
        in_specs=[hbm] * 5,
        out_specs=(hbm,) * 4,
        scratch_shapes=scratch,
        compiler_params=pltpu.CompilerParams(
            collective_id=0, has_side_effects=True, vmem_limit_bytes=58 * 1024 * 1024
        ),
        name="attention_grads",
    )(queries, keys, values, out_grad, out_weight)
    return pl.pallas_call(
        hand_on,
        out_shape=shapes,
        in_specs=[hbm] * 4,
        out_specs=(hbm,) * 4,
        scratch_shapes=[vmem(s.shape, BF16) for s in shapes] + [dma((2, 4))],
        name="hand_on",
    )(*grads)


def solution(mesh):
    return jax.shard_map(
        shards,
        mesh=mesh,
        in_specs=(
            P("context", "mp"),
            P("context", "mp"),
            P("context", "mp"),
            P(("context", "mp"), None),
            P(None, "mp"),
        ),
        out_specs=(P("context", "mp"), P("context", "mp"), P("context", "mp"), P("context", "mp")),
        check_vma=False,
    )
```

time: 104 us -> 75.1 us (0.72)
  Pallas kernels: 96.1 us -> 74.4 us
  local copies, waits for them, and re-layouts: 6.74 us -> 0 us
    pallas_call x1 -> x2, Pallas kernels: 96.1 us -> 74.4 us  [the longest x1 72.1 us: shards(): pl.pallas_call(kernel, out_shape=shapes, in_specs=[hbm] * 5, out_specs=(h...]
    unnamed x4 -> x0, local copies, waits for them, and re-layouts: 6.74 us -> none
where the time goes in v2:
time: 75.1 us; the launch traced here: 75 us
  Pallas kernels  74.4 us (99%)
    pallas_call x1, Pallas kernels, shards(): pl.pallas_call(kernel, out_shape=shapes, in_specs=[hbm] * 5, out_specs=(h...  72.1 us
    pallas_call x1, Pallas kernels, shards(): pl.pallas_call(hand_on, out_shape=shapes, in_specs=[hbm] * 4, out_specs=(...  2.27 us

profile of v2, /device:TPU:1, one launch (start us, length us, event | category | flops | bytes accessed | tf_op | source)
XLA Modules:
  0.0 75.0 jit_solution(17312756613207457895)
XLA Ops:
  0.6 72.1 %attention_grads.1 = (bf16[1024,256]{1,0:T(8,128)(2,1)}, bf16[1024,128]{1,0:T(8,128)(2,1)}, bf16[1024,128]{1,0:T(8,128)(2,1)}, bf16[168,256]{1,0:T(8,128)(2,1)}) custom-call(bf16[1024,256]{1,0:T(8,128)(2,1)} %q_hbm.1, bf16[1024,128]{1,0:T(8,128)(2,1)} %k_hbm.1, bf16[1024,128]{1,0:T(8,128)(2,1)} %v_hbm.1, bf16[128,5376]{1,0:T(8,128)(2,1)} %g_hbm.1, ...), custom_call_target="tpu_custom_call" | custom-call | tf_op jit(solution)/shard_map/attention_grads/pallas_call | solution.py:405
  72.8 2.3 %hand_on.1 = (bf16[1024,256]{1,0:T(8,128)(2,1)}, bf16[1024,128]{1,0:T(8,128)(2,1)}, bf16[1024,128]{1,0:T(8,128)(2,1)}, bf16[168,256]{1,0:T(8,128)(2,1)}) custom-call(bf16[1024,256]{1,0:T(8,128)(2,1)} %get-tuple-element.8.refs_0_, bf16[1024,128]{1,0:T(8,128)(2,1)} %get-tuple-element.9.refs_1_, bf16[1024,128]{1,0:T(8,128)(2,1)} %get-tuple-element.10.refs_2_, ...), custom_call_target="tpu_custom_call" | custom-call | tf_op jit(solution)/shard_map/hand_on/pallas_call | solution.py:416

commit v3 on v2

--- a/solution.py
+++ b/solution.py
@@ -26,6 +26,9 @@
 ENDS = tuple(-(-BLOCK * (s + 1) // 128) * 128 for s in range(STEPS))
 BEGINS = (0,) + ENDS[:-1]
 AHEAD = 2
+AWAY = (4, -3, 3, -2, 2, -1, 1, 0)
+ADDS = ((), (), (0,), (1,), (2,), (3,), (4,), (5, 6))
+PAIR = 2 * ROWS
 
 
 def nt(a, b):
@@ -41,10 +44,10 @@
 
 
 def kernel(
-    q_hbm, k_hbm, v_hbm, g_hbm, w_hbm, dq_hbm, dk_hbm, dv_hbm, dw_hbm,
-    q, kf, vf, kt, vt, gown, g, wp, wf, wb, prob, at, do, dka, dva, wt,
-    as_, bs_, ar, br, sx, fs, fr, hs, hr, dqv, dkv, dvv, dwv,
-    lsem, osem, ag_s, ag_r, halo_s, halo_r, za_s, za_r, zb_s, zb_r, x_s, x_r, back_s, back_r,
+    q_hbm, k_hbm, v_hbm, g_hbm, w_hbm, dqv, dkv, dvv, dwv,
+    q, kf, vf, kt, vt, gown, g, wp, wf, wb, prob, at, do, dn, dka, dva, wt,
+    as_, bs_, ar, br, sx, fs, fr, hs, hr,
+    lsem, ag_s, ag_r, halo_s, halo_r, za_s, za_r, zb_s, zb_r, x_s, x_r, back_s, back_r,
 ):
     c = lax.axis_index("context")
     m = lax.axis_index("mp")
@@ -60,7 +63,8 @@
     below = x * ZS + (z + ZS - 1) % ZS
 
     def target_z(z, step, i):
-        return (z + ZS - 1 - step) % ZS if i < 2 else (z + 1 + step) % ZS
+        away = AWAY[step] if i < 2 else -AWAY[step]
+        return (z + away + ZS) % ZS
 
     local = [
         pltpu.make_async_copy(g_hbm, gown, lsem.at[0]),
@@ -136,7 +140,7 @@
         arrive(step, 1)
         start(step, 3, 6)
         if step + AHEAD < STEPS:
-            start(step + AHEAD, 0, 1, 4)
+            start(step + AHEAD, 0, 1)
 
     def service_far(step):
         arrive(step, 2)
@@ -158,6 +162,8 @@
     reorder(BEGINS[1], ENDS[1])
     start(1, 0, 1, 4)
     reorder(BEGINS[2], ENDS[STEPS - 1])
+    for step in range(2, STEPS):
+        start(step, 4)
 
     def keys_of(b):
         return pl.ds(pl.multiple_of(b * ROWS, ROWS), SPAN)
@@ -217,43 +223,45 @@
     local[4].wait()
     wf[...] = wp[...].astype(F32)
 
-    @pl.loop(0, STEPS)
-    def _(step):
+    for step in range(STEPS):
         for half in (0, 2):
             two = []
             for i in (half, half + 1):
                 p = i * ZS + target_z(z, step, i)
                 two.append(wf[pl.ds(pl.multiple_of(p * PIECE, 8), PIECE), :])
-            rows = pl.ds(pl.multiple_of(step * BLOCK + half * PIECE, 16), 2 * PIECE)
-            wb[rows, :] = jnp.concatenate(two, 0).astype(BF16)
+            begin = step * BLOCK + half * PIECE
+            wb[begin : begin + 2 * PIECE, :] = jnp.concatenate(two, 0).astype(BF16)
 
     def dout_part(step):
-        cols = slice(BEGINS[step], ENDS[step])
-
-        @pl.loop(0, 4)
-        def _(t):
-            rows = pl.ds(pl.multiple_of(t * 256, 256), 256)
-            part = nn(g[rows, cols], wb[cols, :])
-            if step == 0:
-                do[rows, :] = part
-            else:
-                do[rows, :] += part
-
+        part = nn(g[:, BEGINS[step] : ENDS[step]], wb[BEGINS[step] : ENDS[step], :])
+        if step == 0:
+            do[...] = part
+        else:
+            do[...] += part
+
+    def pair_rows(chip):
+        return pl.ds(pl.multiple_of(chip * PAIR, PAIR), PAIR)
+
+    dka[...] = jnp.zeros_like(dka)
+    dva[...] = jnp.zeros_like(dva)
     z_copies = []
 
-    def weight_part(step):
+    def weight_product(step):
         first = step * BLOCK // 128 * 128
         for o in range(0, WIDE, 256):
             part = nn(at[...], g[:, first + o : first + o + 256])
             wt[o : o + 256, :] = jnp.transpose(part, (1, 0))
-        if step > 0:
-            for copy in z_copies[-2:]:
+
+    def weight_sums(step):
+        first = step * BLOCK // 128 * 128
+        for before in ADDS[step]:
+            for copy in z_copies[2 * before : 2 * before + 2]:
                 copy.wait_recv()
         for i in range(XS):
             begin = step * BLOCK - first + i * PIECE
             t = wt[begin : begin + PIECE, :]
-            if step > 0:
-                t = t + (ar[step - 1, i] if i < 2 else br[step - 1, i - 2]).astype(F32)
+            for before in ADDS[step]:
+                t = t + (ar[before, i] if i < 2 else br[before, i - 2]).astype(F32)
             if step == STEPS - 1:
                 sx[i] = t
                 fs[i] = t.astype(BF16)
@@ -262,31 +270,15 @@
             else:
                 bs_[step, i - 2] = t.astype(BF16)
         if step < STEPS - 1:
-            z_copies.append(remote(as_.at[step], ar.at[step], za_s.at[step], za_r.at[step], (above, m)))
-            z_copies.append(remote(bs_.at[step], br.at[step], zb_s.at[step], zb_r.at[step], (below, m)))
+            one, other = (above, below) if AWAY[step] > 0 else (below, above)
+            z_copies.append(remote(as_.at[step], ar.at[step], za_s.at[step], za_r.at[step], (one, m)))
+            z_copies.append(remote(bs_.at[step], br.at[step], zb_s.at[step], zb_r.at[step], (other, m)))
             for copy in z_copies[-2:]:
                 copy.start()
 
-    for step in range(STEPS):
-        if step > 0:
-            service_far(step)
-        if 0 < step < STEPS - 1:
-            service_near(step + 1)
-        arrive(step, 4, 5, 6, 7, 8)
-        weight_part(step)
-        if step < STEPS - 1:
-            dout_part(step)
-
-    x_copies = []
-    for e in (2, 1, 3):
-        to = (x + e) % XS
-        x_copies.append(remote(fs.at[to], fr.at[e - 1], x_s.at[e - 1], x_r.at[e - 1], (to * ZS + z, m)))
-        x_copies[-1].start()
-    dout_part(STEPS - 1)
-
-    def backward(b):
+    def backward(b, dout, first):
         qb = query_rows(b)
-        block = do[rows_at(b), :].astype(BF16)
+        block = dout[pl.ds(pl.multiple_of(first, ROWS), ROWS), :].astype(BF16)
         db = jnp.concatenate([block[:, :128], block[:, 128:]], 0)
         dt = jnp.transpose(db.astype(F32), (1, 0))
         a = jnp.concatenate([at[:128, rows_at(b)], at[128:, rows_at(b)]], 1).astype(F32)
@@ -299,32 +291,92 @@
         dka[keys_of(b), :] += nn(ds, qb)
         dva[keys_of(b), :] += nn(p.astype(BF16), db)
 
-    dka[...] = jnp.zeros_like(dka)
-    dva[...] = jnp.zeros_like(dva)
-
     def back(b):
         return remote(hs.at[b], hr.at[b], back_s.at[b], back_r.at[b], (left, m))
 
-    @pl.loop(0, 4)
-    def _(b):
-        backward(b)
-        hs[b, 0] = (dka[rows_at(b), :] * SCALE).astype(BF16)
-        hs[b, 1] = dva[rows_at(b), :].astype(BF16)
-        back(b).start()
-
-    @pl.loop(4, 8)
-    def _(b):
-        backward(b)
-
-    outs = [pltpu.make_async_copy(dqv, dq_hbm, osem.at[0])]
-    outs[0].start()
+    def send_back(*pieces):
+        for b in pieces:
+            hs[b, 0] = (dka[rows_at(b), :] * SCALE).astype(BF16)
+            hs[b, 1] = dva[rows_at(b), :].astype(BF16)
+            back(b).start()
+
+    for step in range(STEPS - 1):
+        if step > 0:
+            service_near(step + 1)
+            service_far(step)
+        arrive(step, 5, 6, 7, 8)
+        if step == 0:
+            for later in range(STEPS):
+                arrive(later, 4)
+        weight_product(step)
+        weight_sums(step)
+        if step == STEPS - 2:
+            service_far(step + 1)
+        dout_part(step)
+        if step == 2:
+            dn[...] = nn(g[pair_rows(y), :], wb[...])
+        if step == 3:
+
+            @pl.loop(0, 2)
+            def _(t):
+                backward(y * 2 + t, dn, t * ROWS)
+
+    last = STEPS - 1
+    opposite = (y + 2) % YS
+    near = (y + 1) % 2
+
+    def chip_tokens(chip):
+        cols = slice(BEGINS[last], ENDS[last])
+        do[pair_rows(chip), :] += nn(g[pair_rows(chip), cols], wb[cols, :])
+
+        @pl.loop(0, 2)
+        def _(t):
+            backward(chip * 2 + t, do, chip * PAIR + t * ROWS)
+
+    arrive(last, 5, 6)
+    chip_tokens(near)
+
+    @pl.when(y != 2)
+    def _():
+        send_back(0, 1)
+
+    @pl.when(y < 2)
+    def _():
+        send_back(2, 3)
+
+    arrive(last, 7, 8)
+    do[pair_rows(opposite), :] += nn(
+        g[pair_rows(opposite), BEGINS[last] : ENDS[last]], wb[BEGINS[last] : ENDS[last], :]
+    )
+    backward(opposite * 2, do, opposite * PAIR)
+
+    @pl.when(y == 2)
+    def _():
+        send_back(0)
+
+    backward(opposite * 2 + 1, do, opposite * PAIR + ROWS)
+
+    @pl.when(y == 2)
+    def _():
+        send_back(1)
+
+    @pl.when(y >= 2)
+    def _():
+        send_back(2, 3)
+
+    weight_product(last)
+    weight_sums(last)
+    x_copies = []
+    for e in (2, 1, 3):
+        to = (x + e) % XS
+        x_copies.append(remote(fs.at[to], fr.at[e - 1], x_s.at[e - 1], x_r.at[e - 1], (to * ZS + z, m)))
+        x_copies[-1].start()
+    chip_tokens(near + 2)
     total = sx[x]
     for copy, e in zip(x_copies, (2, 1, 3)):
         copy.wait_recv()
         total = total + fr[e - 1].astype(F32)
     dwv[...] = total.astype(BF16)
-    outs.append(pltpu.make_async_copy(dwv, dw_hbm, osem.at[1]))
-    outs[1].start()
     dkv[:HALO, :] = (dka[HALO:SHARD, :] * SCALE).astype(BF16)
     dvv[:HALO, :] = dva[HALO:SHARD, :].astype(BF16)
     for b in range(4):
@@ -333,29 +385,18 @@
         late = slice(SHARD + b * ROWS, SHARD + (b + 1) * ROWS)
         dkv[rows, :] = (dka[late, :] * SCALE + hr[b, 0].astype(F32)).astype(BF16)
         dvv[rows, :] = (dva[late, :] + hr[b, 1].astype(F32)).astype(BF16)
-    outs.append(pltpu.make_async_copy(dkv, dk_hbm, osem.at[2]))
-    outs.append(pltpu.make_async_copy(dvv, dv_hbm, osem.at[3]))
-    outs[2].start()
-    outs[3].start()
     for step in range(STEPS):
         for kind in range(9):
             ag[step][kind].wait_send()
     for copy in halo + z_copies + x_copies + [back(b) for b in range(4)]:
         copy.wait_send()
-    for copy in outs:
-        copy.wait()
 
 
 def hand_on(*refs):
-    ins, outs, held, sem = refs[:4], refs[4:8], refs[8:12], refs[12]
-    first = [pltpu.make_async_copy(ins[i], held[i], sem.at[0, i]) for i in range(4)]
-    second = [pltpu.make_async_copy(held[i], outs[i], sem.at[1, i]) for i in range(4)]
-    for copy in first:
+    copies = [pltpu.make_async_copy(refs[i], refs[4 + i], refs[8].at[i]) for i in range(4)]
+    for copy in copies:
         copy.start()
-    for i in (3, 1, 2, 0):
-        first[i].wait()
-        second[i].start()
-    for copy in second:
+    for copy in copies:
         copy.wait()
 
 
@@ -376,6 +417,7 @@
         vmem((8, SPAN, 256), F32),
         vmem((256, SHARD), BF16),
         vmem((SHARD, 256), F32),
+        vmem((PAIR, 256), F32),
         vmem((HALO + SHARD, 128), F32),
         vmem((HALO + SHARD, 128), F32),
         vmem((WIDE, 256), F32),
@@ -388,11 +430,7 @@
         vmem((XS - 1, PIECE, 256), BF16),
         vmem((4, 2, ROWS, 128), BF16),
         vmem((4, 2, ROWS, 128), BF16),
-        vmem((SHARD, 256), BF16),
-        vmem((SHARD, 128), BF16),
-        vmem((SHARD, 128), BF16),
-        vmem((PIECE, 256), BF16),
-        dma((5,)), dma((4,)), dma((STEPS, 9)), dma((STEPS, 9)), dma((2,)), dma((2,)),
+        dma((5,)), dma((STEPS, 9)), dma((STEPS, 9)), dma((2,)), dma((2,)),
         dma((7,)), dma((7,)), dma((7,)), dma((7,)), dma((3,)), dma((3,)), dma((4,)), dma((4,)),
     ]
     hbm = pl.BlockSpec(memory_space=pl.ANY)
@@ -404,9 +442,9 @@
     )
     grads = pl.pallas_call(
         kernel,
-        out_shape=shapes,
+        out_shape=tuple(vmem(s.shape, s.dtype) for s in shapes),
         in_specs=[hbm] * 5,
-        out_specs=(hbm,) * 4,
+        out_specs=(pl.BlockSpec(memory_space=vmem),) * 4,
         scratch_shapes=scratch,
         compiler_params=pltpu.CompilerParams(
             collective_id=0, has_side_effects=True, vmem_limit_bytes=58 * 1024 * 1024
@@ -416,11 +454,11 @@
     return pl.pallas_call(
         hand_on,
         out_shape=shapes,
-        in_specs=[hbm] * 4,
+        in_specs=[pl.BlockSpec(memory_space=vmem)] * 4,
         out_specs=(hbm,) * 4,
-        scratch_shapes=[vmem(s.shape, BF16) for s in shapes] + [dma((2, 4))],
+        scratch_shapes=[dma((4,))],
         name="hand_on",
-    )(*grads)
+    )(*[pltpu.with_memory_space_constraint(g, vmem) for g in grads])
 
 
 def solution(mesh):

time: 75.1 us -> 72.8 us (0.969)
  Pallas kernels: 74.4 us -> 71.9 us
    pallas_call x2, Pallas kernels: 74.4 us -> 71.9 us  [the longest x1 70.9 us: shards(): pl.pallas_call(kernel, out_shape=tuple((vmem(s.shape, s.dtype) for s in s...]
where the time goes in v3:
time: 72.8 us; the launch traced here: 72.7 us
  Pallas kernels  71.9 us (99%)
  between operations  0.8 us (1%)
    pallas_call x1, Pallas kernels, shards(): pl.pallas_call(kernel, out_shape=tuple((vmem(s.shape, s.dtype) for s in s...  70.9 us

profile of v3, /device:TPU:1, one launch (start us, length us, event | category | flops | bytes accessed | tf_op | source)
XLA Modules:
  0.0 72.7 jit_solution(128549808977277795)
XLA Ops:
  0.6 70.9 %attention_grads.1 = (bf16[1024,256]{1,0:T(8,128)(2,1)S(1)}, bf16[1024,128]{1,0:T(8,128)(2,1)S(1)}, bf16[1024,128]{1,0:T(8,128)(2,1)S(1)}, bf16[168,256]{1,0:T(8,128)(2,1)S(1)}) custom-call(bf16[1024,256]{1,0:T(8,128)(2,1)} %q_hbm.1, bf16[1024,128]{1,0:T(8,128)(2,1)} %k_hbm.1, bf16[1024,128]{1,0:T(8,128)(2,1)} %v_hbm.1, bf16[128,5376]{1,0:T(8,128)(2,1)} %g_hbm.1, ...), custom_call_target="tpu_custom_call" | custom-call | tf_op jit(solution)/shard_map/attention_grads/pallas_call | solution.py:443
  71.5 1.0 %hand_on.1 = (bf16[1024,256]{1,0:T(8,128)(2,1)}, bf16[1024,128]{1,0:T(8,128)(2,1)}, bf16[1024,128]{1,0:T(8,128)(2,1)}, bf16[168,256]{1,0:T(8,128)(2,1)}) custom-call(bf16[1024,256]{1,0:T(8,128)(2,1)S(1)} %get-tuple-element.8.refs_0_, bf16[1024,128]{1,0:T(8,128)(2,1)S(1)} %get-tuple-element.9.refs_1_, bf16[1024,128]{1,0:T(8,128)(2,1)S(1)} %get-tuple-element.10.refs_2_, ...), custom_call_target="tpu_custom_call" | custom-call | tf_op jit(solution)/shard_map/hand_on/pallas_call | solution.py:454

commit v4 on v3

--- a/solution.py
+++ b/solution.py
@@ -73,8 +73,7 @@
         pltpu.make_async_copy(q_hbm, q, lsem.at[3]),
         pltpu.make_async_copy(w_hbm, wp, lsem.at[4]),
     ]
-    for copy in local:
-        copy.start()
+    local[0].start()
     peers = [(c, up), (c, down), (c, sib), (above, m), (below, m), (right, m), (left, m)]
     peers += [(((x + e) % XS) * ZS + z, m) for e in range(1, XS)]
     barrier = pltpu.get_barrier_semaphore()
@@ -134,13 +133,22 @@
         for kind in kinds:
             ag[step][kind].wait_recv()
 
+    def sent(*steps):
+        for step in steps:
+            for kind in range(9):
+                ag[step][kind].wait_send()
+
     def service_near(step):
         arrive(step, 0)
-        start(step, 2, 5)
+        start(step, 2)
+        if step + AHEAD < STEPS:
+            start(step + AHEAD, 0)
+        start(step, 5)
         arrive(step, 1)
-        start(step, 3, 6)
+        start(step, 3)
         if step + AHEAD < STEPS:
-            start(step + AHEAD, 0, 1)
+            start(step + AHEAD, 1)
+        start(step, 6)
 
     def service_far(step):
         arrive(step, 2)
@@ -153,6 +161,8 @@
         remote(v_hbm.at[pl.ds(SHARD - HALO, HALO)], vf.at[pl.ds(0, HALO)], halo_s.at[1], halo_r.at[1], (right, m)),
     ]
     local[0].wait()
+    for copy in local[1:]:
+        copy.start()
     reorder(BEGINS[0], ENDS[0])
     pl.semaphore_wait(barrier, len(peers))
     start(0, 0, 1)
@@ -313,6 +323,8 @@
         if step == STEPS - 2:
             service_far(step + 1)
         dout_part(step)
+        if step > 1:
+            sent(step - 2)
         if step == 2:
             dn[...] = nn(g[pair_rows(y), :], wb[...])
         if step == 3:
@@ -365,12 +377,16 @@
         send_back(2, 3)
 
     weight_product(last)
+    sent(STEPS - 3, STEPS - 2)
     weight_sums(last)
     x_copies = []
     for e in (2, 1, 3):
         to = (x + e) % XS
         x_copies.append(remote(fs.at[to], fr.at[e - 1], x_s.at[e - 1], x_r.at[e - 1], (to * ZS + z, m)))
         x_copies[-1].start()
+    sent(last)
+    for copy in halo + z_copies:
+        copy.wait_send()
     chip_tokens(near + 2)
     total = sx[x]
     for copy, e in zip(x_copies, (2, 1, 3)):
@@ -385,10 +401,7 @@
         late = slice(SHARD + b * ROWS, SHARD + (b + 1) * ROWS)
         dkv[rows, :] = (dka[late, :] * SCALE + hr[b, 0].astype(F32)).astype(BF16)
         dvv[rows, :] = (dva[late, :] + hr[b, 1].astype(F32)).astype(BF16)
-    for step in range(STEPS):
-        for kind in range(9):
-            ag[step][kind].wait_send()
-    for copy in halo + z_copies + x_copies + [back(b) for b in range(4)]:
+    for copy in x_copies + [back(b) for b in range(4)]:
         copy.wait_send()
 
 

time: 72.8 us -> 72.7 us (level)
  no operation moved by 1% of the time
where the time goes in v4:
time: 72.7 us; the launch traced here: 72.6 us
  Pallas kernels  71.8 us (99%)
  between operations  0.8 us (1%)
    pallas_call x1, Pallas kernels, shards(): pl.pallas_call(kernel, out_shape=tuple((vmem(s.shape, s.dtype) for s in s...  70.7 us

profile of v4, /device:TPU:1, one launch (start us, length us, event | category | flops | bytes accessed | tf_op | source)
XLA Modules:
  0.0 72.6 jit_solution(17028960525101538712)
XLA Ops:
  0.6 70.7 %attention_grads.1 = (bf16[1024,256]{1,0:T(8,128)(2,1)S(1)}, bf16[1024,128]{1,0:T(8,128)(2,1)S(1)}, bf16[1024,128]{1,0:T(8,128)(2,1)S(1)}, bf16[168,256]{1,0:T(8,128)(2,1)S(1)}) custom-call(bf16[1024,256]{1,0:T(8,128)(2,1)} %q_hbm.1, bf16[1024,128]{1,0:T(8,128)(2,1)} %k_hbm.1, bf16[1024,128]{1,0:T(8,128)(2,1)} %v_hbm.1, bf16[128,5376]{1,0:T(8,128)(2,1)} %g_hbm.1, ...), custom_call_target="tpu_custom_call" | custom-call | tf_op jit(solution)/shard_map/attention_grads/pallas_call | solution.py:456
  71.4 1.0 %hand_on.1 = (bf16[1024,256]{1,0:T(8,128)(2,1)}, bf16[1024,128]{1,0:T(8,128)(2,1)}, bf16[1024,128]{1,0:T(8,128)(2,1)}, bf16[168,256]{1,0:T(8,128)(2,1)}) custom-call(bf16[1024,256]{1,0:T(8,128)(2,1)S(1)} %get-tuple-element.8.refs_0_, bf16[1024,128]{1,0:T(8,128)(2,1)S(1)} %get-tuple-element.9.refs_1_, bf16[1024,128]{1,0:T(8,128)(2,1)S(1)} %get-tuple-element.10.refs_2_, ...), custom_call_target="tpu_custom_call" | custom-call | tf_op jit(solution)/shard_map/hand_on/pallas_call | solution.py:467
